TPU v7x, 512 devices: a whole 4x4x16 slice. The times are simulated.
512 devices in a mesh: seq: 4 (over z_lo), fsdp: 32 (over z_hi, y, core), dp: 4 (over x).
Axes of the slice: x: 4, y: 4, z: 16 (z_hi: 4, z_lo: 4; z = z_hi * 4 + z_lo), core: 2. Of those that a mesh axis runs over, the one named last changes fastest.
Arguments:
- query: bfloat16 [128, 768, 1024], P(('fsdp', 'dp'), 'seq'), may hold values from -6 to 6
- key: bfloat16 [128, 768, 1024], P(('fsdp', 'dp'), 'seq'), may hold values from -6 to 6
- value: bfloat16 [128, 768, 1024], P(('fsdp', 'dp'), 'seq'), may hold values from -4 to 4
- out_weight: bfloat16 [1024, 2048], P('fsdp'), may hold values from -0.1875 to 0.1875
- out_grad: bfloat16 [128, 768, 2048], P(('fsdp', 'dp'), 'seq'), may hold values from -5 to 5
- block_ids: int32 [8], P('seq'), may hold values from 0 to 7, as said below
Outputs:
- query_grad: bfloat16 [128, 768, 1024], P(('fsdp', 'dp'), 'seq')
- key_grad: bfloat16 [128, 768, 1024], P(('fsdp', 'dp'), 'seq')
- value_grad: bfloat16 [128, 768, 1024], P(('fsdp', 'dp'), 'seq')
- weight_grad: bfloat16 [1024, 2048], P('fsdp')
Inputs may be any that keep to these rules, and one draw needn't show every extreme that they name: `block_ids`: each number 0 to 7 appears once, and entries 2 i and 2 i + 1 always sum to 7.
All inputs are finite; a program needn't handle non-finite values.
Results may differ from a plain program's by a relative error of at most 0.027.
Values may be sent and summed in bfloat16 or wider, within the bound.
No kernel may reach another device: no remote copies, remote signals or barrier semaphores. Data moves between devices by JAX's collectives and lax.ppermute only.
A program may use at most 64 MiB of HBM per device.

v0:
```python
import math
import jax
import jax.numpy as jnp
from jax import lax
from jax.sharding import PartitionSpec as P

HEADS = 8
HD = 128


def positions_of(block_list, block_rows):
    offsets = jnp.arange(block_rows, dtype=jnp.int32)
    return (block_list[:, None] * block_rows + offsets[None, :]).reshape(-1)


def shards(query, key, value, out_weight, out_grad, block_ids):
    tokens_here = query.shape[1]
    width_heads = query.shape[2]
    block_rows = tokens_here // block_ids.shape[0]
    score_scale = 1.0 / math.sqrt(HD)
    all_blocks = lax.all_gather(block_ids, "seq", axis=0, tiled=True)
    query_pos = positions_of(block_ids, block_rows)
    every_pos = positions_of(all_blocks, block_rows)
    key_all, value_all = (
        lax.all_gather(key, "seq", axis=1, tiled=True),
        lax.all_gather(value, "seq", axis=1, tiled=True),
    )
    query_heads = query[0].reshape(tokens_here, HEADS, HD)
    key_heads = key_all[0].reshape(-1, HEADS, HD)
    value_heads = value_all[0].reshape(-1, HEADS, HD)
    scores = (
        jnp.einsum("thd,khd->htk", query_heads, key_heads, preferred_element_type=jnp.float32)
        * score_scale
    )
    allowed = every_pos[None, :] <= query_pos[:, None]
    scores = jnp.where(allowed[None], scores, -jnp.inf)
    row_top = jnp.max(scores, axis=2, keepdims=True)
    row_total = jnp.sum(jnp.exp(scores - row_top), axis=2, keepdims=True)
    log_total = row_top + jnp.log(row_total)
    weights = jnp.exp(scores - log_total)
    weights_low = weights.astype(jnp.bfloat16)
    attended = jnp.einsum(
        "htk,khd->thd", weights_low, value_heads, preferred_element_type=jnp.float32
    ).astype(jnp.bfloat16)
    grad_rows = out_grad[0]
    attn_grad = lax.dot_general(
        grad_rows,
        lax.all_gather(out_weight, "fsdp", axis=0, tiled=True),
        (((1,), (1,)), ((), ())),
        preferred_element_type=jnp.float32,
    ).astype(jnp.bfloat16)
    attended_flat = attended.reshape(tokens_here, width_heads)
    weight_shard = lax.psum_scatter(
        lax.dot_general(
            attended_flat, grad_rows, (((0,), (0,)), ((), ())), preferred_element_type=jnp.float32
        ).astype(jnp.bfloat16),
        "fsdp",
        scatter_dimension=0,
        tiled=True,
    ).astype(jnp.float32)
    token_count = tokens_here * lax.axis_size("seq") * lax.axis_size("fsdp") * lax.axis_size("dp")
    weight_grad = (lax.psum(weight_shard, ("seq", "dp")) * (1.0 / math.sqrt(token_count))).astype(
        jnp.bfloat16
    )
    grad_heads = attn_grad.reshape(tokens_here, HEADS, HD)
    row_delta = jnp.einsum("thd,thd->ht", grad_heads, attended, preferred_element_type=jnp.float32)
    prob_grad = jnp.einsum(
        "thd,khd->htk", grad_heads, value_heads, preferred_element_type=jnp.float32
    )
    score_grad = (weights * (prob_grad - row_delta[:, :, None])).astype(jnp.bfloat16)
    query_grad = (
        jnp.einsum("htk,khd->thd", score_grad, key_heads, preferred_element_type=jnp.float32)
        * score_scale
    ).astype(jnp.bfloat16)
    query_all, grad_all = (
        lax.all_gather(query, "seq", axis=1, tiled=True),
        lax.all_gather(attn_grad[None], "seq", axis=1, tiled=True),
    )
    totals_all, deltas_all = (
        lax.all_gather(log_total[:, :, 0][None], "seq", axis=2, tiled=True),
        lax.all_gather(row_delta[None], "seq", axis=2, tiled=True),
    )
    local_keys = key[0].reshape(tokens_here, HEADS, HD)
    local_values = value[0].reshape(tokens_here, HEADS, HD)
    gathered_queries = query_all[0].reshape(-1, HEADS, HD)
    gathered_grads = grad_all[0].reshape(-1, HEADS, HD)
    back_scores = (
        jnp.einsum("khd,qhd->hkq", local_keys, gathered_queries, preferred_element_type=jnp.float32)
        * score_scale
    )
    back_allowed = query_pos[:, None] <= every_pos[None, :]
    back_scores = jnp.where(back_allowed[None], back_scores, -jnp.inf)
    back_weights = jnp.exp(back_scores - totals_all[0][:, None, :])
    back_low = back_weights.astype(jnp.bfloat16)
    back_prob_grad = jnp.einsum(
        "qhd,khd->hkq", gathered_grads, local_values, preferred_element_type=jnp.float32
    )
    back_score_grad = (back_weights * (back_prob_grad - deltas_all[0][:, None, :])).astype(
        jnp.bfloat16
    )
    key_grad = (
        jnp.einsum(
            "hkq,qhd->khd", back_score_grad, gathered_queries, preferred_element_type=jnp.float32
        )
        * score_scale
    ).astype(jnp.bfloat16)
    value_grad = jnp.einsum(
        "hkq,qhd->khd", back_low, gathered_grads, preferred_element_type=jnp.float32
    ).astype(jnp.bfloat16)
    return (
        query_grad.reshape(tokens_here, width_heads)[None],
        key_grad.reshape(tokens_here, width_heads)[None],
        value_grad.reshape(tokens_here, width_heads)[None],
        weight_grad,
    )


def solution(mesh):
    in_specs = (
        P(("fsdp", "dp"), "seq", None),
        P(("fsdp", "dp"), "seq", None),
        P(("fsdp", "dp"), "seq", None),
        P("fsdp", None),
        P(("fsdp", "dp"), "seq", None),
        P("seq"),
    )
    out_specs = (
        P(("fsdp", "dp"), "seq", None),
        P(("fsdp", "dp"), "seq", None),
        P(("fsdp", "dp"), "seq", None),
        P("fsdp", None),
    )
    return jax.shard_map(shards, mesh=mesh, in_specs=in_specs, out_specs=out_specs, check_vma=False)
```

profile of v0, /device:TPU:16, one launch (start us, length us, event | category | flops | bytes accessed | tf_op | source)
XLA Modules:
  0.0 531.4 jit_solution(5790894048885190867)
XLA Ops:
  8.0 0.7 all-gather.11.cloned.1.call-update
  10.0 1.3 dynamic-slice
  12.0 0.9 dynamic-update-slice
  12.8 9.1 %all-reduce = s32[8]{0:T(128)S(1)} all-reduce(s32[8]{0:T(128)S(1)} %dynamic-update-slice), channel_id=1, replica_groups=mesh['seq'=4,'fsdp'=32,'dp'=4] {'seq'}, use_global_device_ids=true, to_apply=%add | all-reduce | flops 8 | bytes 64
  22.9 1.1 copy.64
  24.0 86.7 %all-gather.13.cloned.1.call-done = bf16[1024,2048]{1,0:T(8,128)(2,1)} async-done(((bf16[32,2048]{1,0:T(8,128)(2,1)}), bf16[1024,2048]{1,0:T(8,128)(2,1)}) %all-gather.13.cloned.1.call-update) | async-done | bytes 4194320 | tf_op jit(solution)/shard_map/all_gather | solution.py:48
  110.6 4.5 convolution_convert_fusion.1
  115.4 39.8 %all-gather.11.cloned.1.call-done = bf16[1,768,1024]{2,1,0:T(8,128)(2,1)} async-done(((bf16[1,192,1024]{2,1,0:T(8,128)(2,1)}), bf16[1,768,1024]{2,1,0:T(8,128)(2,1)}) %all-gather.11.cloned.1.call-update) | async-done | bytes 1572880 | tf_op jit(solution)/shard_map/all_gather | solution.py:25
  155.2 1.7 copy.28
  157.0 46.7 %all-gather.15.cloned.1.call-done = bf16[1,768,1024]{2,1,0:T(8,128)(2,1)} async-done(((bf16[1,192,1024]{2,1,0:T(8,128)(2,1)}), bf16[1,768,1024]{2,1,0:T(8,128)(2,1)}) %all-gather.15.cloned.1.call-update) | async-done | bytes 1572880 | tf_op jit(solution)/shard_map/all_gather | solution.py:26
  203.7 2.6 copy.31
  206.3 1.0 fusion.3
  207.3 1.2 exponential_reduce_fusion
  208.7 1.1 copy-done.3
  209.9 1.6 multiply_reduce_fusion
  211.6 3.4 convolution_convert_fusion
  215.0 0.8 copy.67
  215.9 13.1 %all-gather.3 = f32[4,192,8]{1,2,0:T(8,128)S(1)} all-gather(f32[1,192,8]{1,2,0:T(8,128)S(1)} %bitcast.115), channel_id=2, replica_groups=mesh['seq'=4,'fsdp'=32,'dp'=4] {'seq'}, dimensions={0}, use_global_device_ids=true | all-gather | bytes 30720 | tf_op jit(solution)/shard_map/all_gather | solution.py:80
  229.1 22.9 %all-gather.17.cloned.1.call-done = bf16[1,768,1024]{2,1,0:T(8,128)(2,1)} async-done(((bf16[1,192,1024]{2,1,0:T(8,128)(2,1)}), bf16[1,768,1024]{2,1,0:T(8,128)(2,1)}) %all-gather.17.cloned.1.call-update) | async-done | bytes 1572880 | tf_op jit(solution)/shard_map/all_gather | solution.py:76
  252.0 1.7 copy.37
  253.7 2.9 fusion.72
  256.7 6.3 %fusion.56 = bf16[192,8,128]{2,0,1:T(8,128)(2,1)} fusion(bf16[768,8,128]{0,2,1:T(8,128)(2,1)} %bitcast.105, f32[8,192,768]{2,1,0:T(8,128)} %copy-done.1, f32[8,192]{1,0:T(8,128)S(1)} %get-tuple-element.8, f32[8,192]{1,0:T(8,128)S(1)} %log_add_fusion, pred[192,768]{1,0:T(8,128)(4,1)S(1)} %get-tuple-element.5, bf16[768,8,128]{0,2,1:T(8,128)(2,1)} %bitcast.106, ...), kind=kOutput, calls=%fused_computation.39 | convolution fusion | flops 611450880 | bytes 8810496 | tf_op jit(solution)/shard_map/htk,khd->thd/dot_general | solution.py:72
  262.9 1.3 copy.36
  264.2 0.9 broadcast_in_dim_reshape.6
  265.1 13.4 %all-gather.4 = f32[4,192,8]{1,2,0:T(8,128)S(1)} all-gather(f32[1,192,8]{1,2,0:T(8,128)S(1)} %bitcast.119), channel_id=4, replica_groups=mesh['seq'=4,'fsdp'=32,'dp'=4] {'seq'}, dimensions={0}, use_global_device_ids=true | all-gather | bytes 30720 | tf_op jit(solution)/shard_map/all_gather | solution.py:81
  278.6 22.4 %all-gather.19.cloned.1.call-done = bf16[768,1024]{1,0:T(8,128)(2,1)} async-done(((bf16[192,1024]{1,0:T(8,128)(2,1)}), bf16[768,1024]{1,0:T(8,128)(2,1)}) %all-gather.19.cloned.1.call-update) | async-done | bytes 1572880 | tf_op jit(solution)/shard_map/all_gather | solution.py:77
  301.0 4.8 fusion.51
  306.1 0.9 broadcast_in_dim_reshape.14
  307.0 4.2 fusion.57
  311.5 0.9 broadcast_in_dim_reshape.15
  312.4 129.9 %reduce-scatter.2.cloned.1.call-done = bf16[32,2048]{1,0:T(8,128)(2,1)} async-done(((bf16[1024,2048]{1,0:T(8,128)(2,1)}), bf16[32,2048]{1,0:T(8,128)(2,1)}) %reduce-scatter.2.cloned.1.call-update) | async-done | bytes 131088 | tf_op jit(solution)/shard_map/reduce_scatter | solution.py:53
  442.3 81.5 %all-reduce.2 = f32[32,2048]{1,0:T(8,128)S(1)} all-reduce(bf16[32,2048]{1,0:T(8,128)(2,1)} %reduce-scatter.2.cloned.1.call-done), channel_id=1, replica_groups=mesh['seq'=4,'fsdp'=32,'dp'=4] {'seq','dp'}, use_global_device_ids=true, to_apply=%region_3.4 | all-reduce | flops 65536 | bytes 393216 | tf_op jit(solution)/shard_map/psum | solution.py:62
  (45 shorter events, 5.0 us)
Async XLA Ops:
  7.2 103.5 %copy-start = (bf16[1,192,2048]{2,1,0:T(8,128)(2,1)S(1)}, bf16[1,192,2048]{2,1,0:T(8,128)(2,1)}, u32[]{:S(2)}) copy-start(bf16[1,192,2048]{2,1,0:T(8,128)(2,1)} %param.10) | copy-start | bytes 2359300
  7.2 103.5 %all-gather.13.cloned.1.call-start = ((), (), s32[]{:S(2)}) async-start(), calls=%async_computation.2 | async-start | bytes 4325376 | tf_op jit(solution)/shard_map/all_gather | solution.py:48
  7.9 147.3 %all-gather.11.cloned.1.call-start = ((), (), s32[]{:S(2)}) async-start(), calls=%async_computation.1 | async-start | bytes 1966080 | tf_op jit(solution)/shard_map/all_gather | solution.py:25
  8.7 195.0 %all-gather.15.cloned.1.call-start = ((), (), s32[]{:S(2)}) async-start(), calls=%async_computation.3 | async-start | bytes 1966080 | tf_op jit(solution)/shard_map/all_gather | solution.py:26
  9.4 242.6 %all-gather.17.cloned.1.call-start = ((), (), s32[]{:S(2)}) async-start(), calls=%async_computation.4 | async-start | bytes 1966080 | tf_op jit(solution)/shard_map/all_gather | solution.py:76
  10.0 291.0 %all-gather.19.cloned.1.call-start = ((), (), s32[]{:S(2)}) async-start(), calls=%async_computation.6 | async-start | bytes 1966080 | tf_op jit(solution)/shard_map/all_gather | solution.py:77
  115.1 327.2 %reduce-scatter.2.cloned.1.call-start = ((), (), s32[]{:S(2)}) async-start(), calls=%async_computation.5 | async-start | bytes 4325376 | tf_op jit(solution)/shard_map/reduce_scatter | solution.py:53
  156.9 50.3 %copy-start.2 = (bf16[1,768,1024]{1,2,0:T(8,128)(2,1)}, bf16[1,768,1024]{1,2,0:T(8,128)(2,1)S(1)}, u32[]{:S(2)}) copy-start(bf16[1,768,1024]{1,2,0:T(8,128)(2,1)S(1)} %copy.28) | copy-start | bytes 4718596
  206.3 2.3 copy-start.6
  207.3 4.2 copy-start.1
  207.3 2.6 copy-start.3
  211.5 3.4 copy-start.4
  211.5 3.5 copy-start.5
  256.7 44.3 %copy-start.7 = (bf16[24,8,8,128]{3,2,1,0:T(8,128)(2,1)S(1)}, bf16[24,8,8,128]{3,2,1,0:T(8,128)(2,1)}, u32[]{:S(2)}) copy-start(bf16[24,8,8,128]{3,2,1,0:T(8,128)(2,1)} %copy.67) | copy-start | bytes 1179652
Sparse Core Ops, SparseCore 0:
  11.1 99.4 all-gather.12
  112.7 42.4 all-gather.10
  157.3 46.2 all-gather.14
  205.6 46.3 all-gather.16
  254.5 46.4 all-gather.18
  305.4 136.9 reduce-scatter.1
where the time goes:
time: 532 us; the launch traced here: 531 us
  waiting for transfers between devices  351 us (66%)
  blocking collectives  117 us (22%)
  matrix products  28.8 us (5%)
  local copies, waits for them, and re-layouts  16.2 us (3%)
  between operations  15 us (3%)
    reduce_scatter x1, waiting for transfers between devices, shards(): lax.psum_scatter(lax.dot_general(attended_flat, grad_rows, (((0,), (0,)),...  130 us
    all_gather x1, waiting for transfers between devices, shards(): lax.all_gather(out_weight, 'fsdp', axis=0, tiled=True)  86.7 us
    psum x1, blocking collectives, shards(): lax.psum(weight_shard, ('seq', 'dp')) * (1.0 / math.sqrt(token_count))  81.5 us
    all_gather x1, waiting for transfers between devices, shards(): lax.all_gather(value, 'seq', axis=1, tiled=True)  46.7 us
    all_gather x1, waiting for transfers between devices, shards(): lax.all_gather(key, 'seq', axis=1, tiled=True)  39.8 us
    all_gather x1, waiting for transfers between devices, shards(): lax.all_gather(query, 'seq', axis=1, tiled=True)  22.9 us
    all_gather x1, waiting for transfers between devices, shards(): lax.all_gather(attn_grad[None], 'seq', axis=1, tiled=True)  22.4 us
    all_gather x1, blocking collectives, shards(): lax.all_gather(row_delta[None], 'seq', axis=2, tiled=True)  13.4 us
  transfers between devices with their start and end apart: 6, of which 6 were waited for; matrix products, arithmetic and copies ran while one was open for 9% of the time, Pallas kernels for 0%

commit v1 on v0

--- a/solution.py
+++ b/solution.py
@@ -74,7 +74,9 @@
     ).astype(jnp.bfloat16)
     query_all, grad_all = (
         lax.all_gather(query, "seq", axis=1, tiled=True),
-        lax.all_gather(attn_grad[None], "seq", axis=1, tiled=True),
+        jnp.concatenate(
+            lax.all_to_all(jnp.stack([attn_grad[None]] * lax.axis_size("seq")), "seq", 0, 0), axis=1
+        ),
     )
     totals_all, deltas_all = (
         lax.all_gather(log_total[:, :, 0][None], "seq", axis=2, tiled=True),

time: 532 us -> 511 us (0.961)
  the two profiles are of different devices: /device:TPU:16 before, /device:TPU:8 now
where the time goes in v1:
time: 511 us
  waiting for transfers between devices  264 us (52%)
  blocking collectives  169 us (33%)
  matrix products  33.6 us (7%)
  local copies, waits for them, and re-layouts  18.6 us (4%)
  between operations  14.6 us (3%)
  other arithmetic  6.07 us (1%)
    all_gather x1, waiting for transfers between devices, shards(): lax.all_gather(out_weight, 'fsdp', axis=0, tiled=True)  91.5 us
    reduce_scatter x1, waiting for transfers between devices, shards(): lax.psum_scatter(lax.dot_general(attended_flat, grad_rows, (((0,), (0,)),...  90.3 us
    psum x1, blocking collectives, shards(): lax.psum(weight_shard, ('seq', 'dp')) * (1.0 / math.sqrt(token_count))  81.2 us
    all_gather x1, blocking collectives, shards(): lax.all_gather(log_total[:, :, 0][None], 'seq', axis=2, tiled=True)  65.9 us
    all_gather x1, waiting for transfers between devices, shards(): lax.all_gather(value, 'seq', axis=1, tiled=True)  43.6 us
    all_gather x1, waiting for transfers between devices, shards(): lax.all_gather(key, 'seq', axis=1, tiled=True)  36.5 us
    all_gather x1, blocking collectives, shards(): lax.all_gather(row_delta[None], 'seq', axis=2, tiled=True)  13.1 us
  transfers between devices with their start and end apart: 6, of which 4 were waited for; matrix products, arithmetic and copies ran while one was open for 11% of the time, Pallas kernels for 0%

profile of v1, /device:TPU:8, one launch (start us, length us, event | category | flops | bytes accessed | tf_op | source)
XLA Modules:
  0.0 510.7 jit_solution(646828153914604682)
XLA Ops:
  8.0 0.7 all-gather.13.cloned.1.call-update
  10.0 1.3 dynamic-slice
  12.0 0.9 dynamic-update-slice
  13.5 9.1 %all-reduce = s32[8]{0:T(128)S(1)} all-reduce(s32[8]{0:T(128)S(1)} %dynamic-update-slice), channel_id=1, replica_groups=mesh['seq'=4,'fsdp'=32,'dp'=4] {'seq'}, use_global_device_ids=true, to_apply=%add | all-reduce | flops 8 | bytes 64
  22.9 1.1 copy.62
  24.0 0.9 broadcast_compare_fusion
  24.9 36.5 %all-gather.9.cloned.1.call-done = bf16[1,768,1024]{2,1,0:T(8,128)(2,1)} async-done(((bf16[1,192,1024]{2,1,0:T(8,128)(2,1)}), bf16[1,768,1024]{2,1,0:T(8,128)(2,1)}) %all-gather.9.cloned.1.call-update) | async-done | bytes 1572880 | tf_op jit(solution)/shard_map/all_gather | solution.py:25
  61.4 1.7 copy.27
  63.1 3.0 fusion.3
  66.1 43.6 %all-gather.13.cloned.1.call-done = bf16[1,768,1024]{2,1,0:T(8,128)(2,1)} async-done(((bf16[1,192,1024]{2,1,0:T(8,128)(2,1)}), bf16[1,768,1024]{2,1,0:T(8,128)(2,1)}) %all-gather.13.cloned.1.call-update) | async-done | bytes 1572880 | tf_op jit(solution)/shard_map/all_gather | solution.py:26
  109.8 2.6 copy.30
  112.4 3.6 exponential_reduce_fusion
  116.0 91.5 %all-gather.11.cloned.1.call-done = bf16[1024,2048]{1,0:T(8,128)(2,1)} async-done(((bf16[32,2048]{1,0:T(8,128)(2,1)}), bf16[1024,2048]{1,0:T(8,128)(2,1)}) %all-gather.11.cloned.1.call-update) | async-done | bytes 4194320 | tf_op jit(solution)/shard_map/all_gather | solution.py:48
  207.5 3.7 convolution_convert_fusion.1
  211.4 3.9 multiply_reduce_fusion
  215.2 3.4 convolution_convert_fusion
  218.7 1.4 stack.3
  220.0 3.8 all-to-all-start
  223.9 0.8 copy.66
  224.7 65.9 %all-gather.2 = f32[4,192,8]{1,2,0:T(8,128)S(1)} all-gather(f32[1,192,8]{1,2,0:T(8,128)S(1)} %bitcast.98), channel_id=2, replica_groups=mesh['seq'=4,'fsdp'=32,'dp'=4] {'seq'}, dimensions={0}, use_global_device_ids=true | all-gather | bytes 30720 | tf_op jit(solution)/shard_map/all_gather | solution.py:82
  291.3 2.6 copy.36
  293.9 4.4 fusion.69
  298.3 5.6 %fusion.53 = bf16[192,8,128]{2,0,1:T(8,128)(2,1)S(1)} fusion(bf16[768,8,128]{0,2,1:T(8,128)(2,1)} %bitcast.86, f32[8,192,768]{2,1,0:T(8,128)} %get-tuple-element.7, f32[8,192]{1,0:T(8,128)S(1)} %get-tuple-element.8, f32[8,192]{1,0:T(8,128)S(1)} %log_add_fusion, pred[192,768]{1,0:T(8,128)(4,1)S(1)} %copy-done.9, bf16[768,8,128]{0,2,1:T(8,128)(2,1)} %bitcast.87, ...), kind=kOutput, calls=%fused_computation.37 | convolution fusion | flops 611450880 | bytes 8810496 | tf_op jit(solution)/shard_map/htk,khd->thd/dot_general | solution.py:72
  304.2 0.9 broadcast_in_dim_reshape.6
  305.1 13.1 %all-gather.3 = f32[4,192,8]{1,2,0:T(8,128)S(1)} all-gather(f32[1,192,8]{1,2,0:T(8,128)S(1)} %bitcast.102), channel_id=3, replica_groups=mesh['seq'=4,'fsdp'=32,'dp'=4] {'seq'}, dimensions={0}, use_global_device_ids=true | all-gather | bytes 30720 | tf_op jit(solution)/shard_map/all_gather | solution.py:83
  318.3 1.6 copy.65
  319.9 5.7 %fusion.48 = bf16[192,8,128]{2,0,1:T(8,128)(2,1)S(1)} fusion(bf16[768,8,128]{0,2,1:T(8,128)(2,1)} %bitcast.84, f32[8,192,768]{2,1,0:T(8,128)} %fusion.69, f32[8,768]{1,0:T(8,128)S(1)} %bitcast.101, f32[8,768]{1,0:T(8,128)} %bitcast.99, pred[192,768]{1,0:T(8,128)(4,1)} %get-tuple-element.4, bf16[768,8,128]{2,1,0:T(8,128)(2,1)} %bitcast.89, ...), kind=kOutput, calls=%fused_computation.36 | convolution fusion | flops 611450880 | bytes 8847360 | tf_op jit(solution)/shard_map/hkq,qhd->khd/dot_general | solution.py:104
  325.9 0.9 broadcast_in_dim_reshape.14
  326.9 3.9 fusion.54
  331.0 0.9 broadcast_in_dim_reshape.15
  331.9 90.3 %reduce-scatter.2.cloned.1.call-done = bf16[32,2048]{1,0:T(8,128)(2,1)} async-done(((bf16[1024,2048]{1,0:T(8,128)(2,1)}), bf16[32,2048]{1,0:T(8,128)(2,1)}) %reduce-scatter.2.cloned.1.call-update) | async-done | bytes 131088 | tf_op jit(solution)/shard_map/reduce_scatter | solution.py:53
  422.2 81.2 %all-reduce.2 = f32[32,2048]{1,0:T(8,128)S(1)} all-reduce(bf16[32,2048]{1,0:T(8,128)(2,1)} %reduce-scatter.2.cloned.1.call-done), channel_id=1, replica_groups=mesh['seq'=4,'fsdp'=32,'dp'=4] {'seq','dp'}, use_global_device_ids=true, to_apply=%region_3.4 | all-reduce | flops 65536 | bytes 393216 | tf_op jit(solution)/shard_map/psum | solution.py:62
  (52 shorter events, 5.6 us)
Async XLA Ops:
  7.2 200.3 %copy-start = (bf16[1,192,2048]{2,1,0:T(8,128)(2,1)S(1)}, bf16[1,192,2048]{2,1,0:T(8,128)(2,1)}, u32[]{:S(2)}) copy-start(bf16[1,192,2048]{2,1,0:T(8,128)(2,1)} %param.10) | copy-start | bytes 2359300
  7.2 54.2 %all-gather.9.cloned.1.call-start = ((), (), s32[]{:S(2)}) async-start(), calls=%async_computation.2 | async-start | bytes 1966080 | tf_op jit(solution)/shard_map/all_gather | solution.py:25
  7.9 101.9 %all-gather.13.cloned.1.call-start = ((), (), s32[]{:S(2)}) async-start(), calls=%async_computation.4 | async-start | bytes 1966080 | tf_op jit(solution)/shard_map/all_gather | solution.py:26
  8.7 198.8 %all-gather.11.cloned.1.call-start = ((), (), s32[]{:S(2)}) async-start(), calls=%async_computation.3 | async-start | bytes 4325376 | tf_op jit(solution)/shard_map/all_gather | solution.py:48
  9.4 281.9 %all-gather.15.cloned.1.call-start = ((), (), s32[]{:S(2)}) async-start(), calls=%async_computation.5 | async-start | bytes 1966080 | tf_op jit(solution)/shard_map/all_gather | solution.py:76
  10.0 412.3 %reduce-scatter.2.cloned.1.call-start = ((), (), s32[]{:S(2)}) async-start(), calls=%async_computation.6 | async-start | bytes 4325376 | tf_op jit(solution)/shard_map/reduce_scatter | solution.py:53
  24.9 186.5 %copy-start.8 = (pred[192,768]{1,0:T(8,128)(4,1)}, pred[192,768]{1,0:T(8,128)(4,1)S(1)}, u32[]{:S(2)}) copy-start(pred[192,768]{1,0:T(8,128)(4,1)S(1)} %get-tuple-element.5) | copy-start | bytes 442372
  63.1 49.3 %copy-start.1 = (bf16[1,768,1024]{1,2,0:T(8,128)(2,1)}, bf16[1,768,1024]{1,2,0:T(8,128)(2,1)S(1)}, u32[]{:S(2)}) copy-start(bf16[1,768,1024]{1,2,0:T(8,128)(2,1)S(1)} %copy.27) | copy-start | bytes 4718596
  116.0 95.4 %copy-start.2 = (bf16[1,768,1024]{1,2,0:T(8,128)(2,1)S(1)}, bf16[1,768,1024]{1,2,0:T(8,128)(2,1)}, u32[]{:S(2)}) copy-start(bf16[1,768,1024]{1,2,0:T(8,128)(2,1)} %copy.30) | copy-start | bytes 4718596
  211.2 7.5 %copy-start.6 = (bf16[192,1024]{1,0:T(8,128)(2,1)}, bf16[192,1024]{1,0:T(8,128)(2,1)S(1)}, u32[]{:S(2)}) copy-start(bf16[192,1024]{1,0:T(8,128)(2,1)S(1)} %convolution_convert_fusion.1) | copy-start | bytes 1179652
  218.6 5.2 %copy-start.4 = (bf16[1,192,1024]{2,1,0:T(8,128)(2,1)S(1)}, bf16[1,192,1024]{2,1,0:T(8,128)(2,1)}, u32[]{:S(2)}) copy-start(bf16[1,192,1024]{2,1,0:T(8,128)(2,1)} %param.7) | copy-start | bytes 1179652
  218.6 5.3 %copy-start.5 = (bf16[1,192,1024]{2,1,0:T(8,128)(2,1)S(1)}, bf16[1,192,1024]{2,1,0:T(8,128)(2,1)}, u32[]{:S(2)}) copy-start(bf16[1,192,1024]{2,1,0:T(8,128)(2,1)} %param.8) | copy-start | bytes 1179652
  220.0 98.3 %all-to-all-start = ((bf16[4,1,192,1024]{3,2,1,0:T(8,128)(2,1)}), bf16[4,1,192,1024]{3,2,1,0:T(8,128)(2,1)S(1)}, u32[]{:S(2)}, u32[]{:S(2)}) async-start(bf16[4,1,192,1024]{3,2,1,0:T(8,128)(2,1)} %stack.3), calls=%async_computation | async-start | bytes 3145728 | tf_op jit(solution)/shard_map/all_to_all | solution.py:78
  291.3 7.0 %copy-start.7 = (bf16[192,1024]{1,0:T(8,128)(2,1)S(1)}, bf16[192,1024]{1,0:T(8,128)(2,1)}, u32[]{:S(2)}) copy-start(bf16[192,1024]{1,0:T(8,128)(2,1)} %copy-done.6) | copy-start | bytes 1179652
  291.3 7.0 %copy-start.9 = (pred[192,768]{1,0:T(8,128)(4,1)S(1)}, pred[192,768]{1,0:T(8,128)(4,1)}, u32[]{:S(2)}) copy-start(pred[192,768]{1,0:T(8,128)(4,1)} %copy-done.8) | copy-start | bytes 442372
  303.9 16.0 %copy-start.10 = (bf16[24,8,8,128]{3,2,1,0:T(8,128)(2,1)S(1)}, bf16[24,8,8,128]{3,2,1,0:T(8,128)(2,1)}, u32[]{:S(2)}) copy-start(bf16[24,8,8,128]{3,2,1,0:T(8,128)(2,1)} %copy.66) | copy-start | bytes 1179652
  319.9 6.9 %copy-start.3 = (bf16[96,8,8,128]{3,2,1,0:T(8,128)(2,1)S(1)}, bf16[96,8,8,128]{3,2,1,0:T(8,128)(2,1)}, u32[]{:S(2)}) copy-start(bf16[96,8,8,128]{3,2,1,0:T(8,128)(2,1)} %copy.65) | copy-start | bytes 4718596
Sparse Core Ops, SparseCore 0:
  10.1 51.1 all-gather.8
  63.4 46.2 all-gather.12
  112.9 94.4 all-gather.10
  209.4 65.5 all-gather.14
  279.4 142.8 reduce-scatter.1
